TPU v7x, 256 devices: a whole 4x4x8 slice. The times are simulated.
256 devices in a mesh: dp: 4 (over y), cp: 64 (over x, z, core).
Axes of the slice: x: 4, y: 4, z: 8, core: 2. Of those that a mesh axis runs over, the one named last changes fastest.
Arguments:
- query_rows: bfloat16 [32768, 4096], P(('dp', 'cp')), parts along dimension 0, may hold values from -90 to 90
- key_rows: bfloat16 [32768, 512], P(('dp', 'cp')), parts along dimension 0, may hold values from -5 to 5
- value_rows: bfloat16 [32768, 512], P(('dp', 'cp')), parts along dimension 0, may hold values from -6 to 6
- gate_rows: bfloat16 [32768, 4096], P(('dp', 'cp')), parts along dimension 0, may hold values from -6 to 6
- doc_ids: int32 [32768], P(('dp', 'cp')), parts along dimension 0, may hold values from 0 to 15, never falling along the last dimension, each value on 1 to 4096 neighbouring positions
- block_lists: int32 [256, 64], P(('dp', 'cp')), parts along dimension 0, may hold values from 0 to 1, as said below
Outputs:
- gated_attention: bfloat16 [32768, 4096], P(('dp', 'cp')), parts along dimension 0
There are 4 independent parts, one for each index of `dp`. A program takes and returns all parts, laid end to end along the dimension named above; each array names one. Nothing has to cross between parts.
Inputs may be any that keep to these rules, and one draw needn't show every extreme that they name: `block_lists`: row q has a 1 at column q and only zeros at columns above q.
All inputs are finite; a program needn't handle non-finite values.
Results may differ from a plain program's by a relative error of at most 0.0038.
Values may be sent and summed in bfloat16 or wider, within the bound.
No kernel may reach another device: no remote copies, remote signals or barrier semaphores. Data moves between devices by JAX's collectives and lax.ppermute only.
A program may use at most 128 MiB of HBM per device.

v0:
```python
import math
import jax
import jax.numpy as jnp
from jax import lax
from jax.sharding import PartitionSpec as P

H = 16
KVH = 2
HD = 256
BLK = 128


def pick_size(length):
    for candidate in (2048, 1024, 512, 256, 128):
        return candidate
    return length


def make_fold(query_rows, positions, query_docs, all_docs, all_lists):
    total_rows = query_rows.shape[0]
    num_blocks = all_lists.shape[0]
    seq_rows = all_docs.shape[0]
    groups = H // KVH
    scale_factor = 1.0 / math.sqrt(HD)
    grouped = query_rows.reshape(total_rows, KVH, groups, HD)
    block_range = jnp.arange(num_blocks, dtype=jnp.int32)
    selector = ((positions // BLK)[:, None] == block_range[None, :]).astype(jnp.bfloat16)
    row_lists = jnp.dot(
        selector, all_lists.astype(jnp.bfloat16), preferred_element_type=jnp.float32
    ).astype(jnp.bfloat16)
    padded_lists = jnp.concatenate(
        [jnp.zeros((total_rows, num_blocks), jnp.bfloat16), row_lists], axis=1
    )
    padded_docs = jnp.concatenate([jnp.full((seq_rows,), -1, jnp.int32), all_docs], axis=0)

    def update(state, key_block, value_block, block_start):
        width = key_block.shape[0]
        key_pos = block_start + jnp.arange(width, dtype=jnp.int32)
        key_docs = lax.dynamic_slice_in_dim(padded_docs, block_start + seq_rows, width)
        block_count = width // BLK
        listed_blocks = lax.dynamic_slice_in_dim(
            padded_lists, block_start // BLK + num_blocks, block_count, 1
        )
        listed = jnp.repeat(listed_blocks, BLK, axis=1)
        visible = (
            (key_pos[None, :] >= 0)
            & (key_pos[None, :] <= positions[:, None])
            & (key_docs[None, :] == query_docs[:, None])
            & (listed > 0.5)
        )

        def compute(inner):
            running_max, running_sum, weighted = inner
            scores = (
                jnp.einsum(
                    "rkgd,nkd->kgrn",
                    grouped,
                    key_block.reshape(width, KVH, HD),
                    preferred_element_type=jnp.float32,
                )
                * scale_factor
            )
            scores = jnp.where(visible[None, None], scores, -1e30)
            new_max = jnp.maximum(running_max, jnp.max(scores, axis=-1))
            weights = jnp.where(visible[None, None], jnp.exp(scores - new_max[..., None]), 0.0)
            decay = jnp.exp(running_max - new_max)
            new_sum = decay * running_sum + jnp.sum(weights, axis=-1)
            product = jnp.einsum(
                "kgrn,nkd->kgrd",
                weights.astype(jnp.bfloat16),
                value_block.reshape(width, KVH, HD),
                preferred_element_type=jnp.float32,
            )
            return (new_max, new_sum, decay[..., None] * weighted + product)

        return lax.cond(jnp.any(visible), compute, lambda inner: inner, state)

    def fold(state, piece, start):
        key_piece, value_piece = piece
        length = key_piece.shape[0]
        step_size = pick_size(length)
        count = length // step_size
        key_steps = key_piece.reshape(count, step_size, key_piece.shape[1])
        value_steps = value_piece.reshape(count, step_size, value_piece.shape[1])
        starts = step_size * jnp.arange(count, dtype=jnp.int32)

        def advance(inner, inputs):
            return (update(inner, inputs[0], inputs[1], inputs[2]), None)

        state, _ = lax.scan(advance, state, (key_steps, value_steps, starts))
        return state

    initial = (
        jnp.full((KVH, groups, total_rows), -1e30, jnp.float32),
        jnp.zeros((KVH, groups, total_rows), jnp.float32),
        jnp.zeros((KVH, groups, total_rows, HD), jnp.float32),
    )
    return (fold, initial)


def finish(state, total_rows):
    running_max, running_sum, weighted = state
    result = weighted / running_sum[..., None]
    return jnp.transpose(result, (2, 0, 1, 3)).reshape(total_rows, H * HD)


def fold_all(fold, initial, key_rows, value_rows):
    return fold(
        initial,
        (
            lax.all_gather(key_rows, "cp", axis=0, tiled=True),
            lax.all_gather(value_rows, "cp", axis=0, tiled=True),
        ),
        jnp.int32(0),
    )


def on_device(query_rows, key_rows, value_rows, gate_rows, doc_ids, block_lists):
    rows_here = query_rows.shape[0]
    position = lax.axis_index("cp")
    all_docs, all_lists = (
        lax.all_gather(doc_ids, "cp", axis=0, tiled=True),
        lax.all_gather(block_lists, "cp", axis=0, tiled=True),
    )
    first_row = position * rows_here
    positions = first_row + jnp.arange(rows_here, dtype=jnp.int32)
    fold, initial = make_fold(query_rows, positions, doc_ids, all_docs, all_lists)
    state = fold_all(fold, initial, key_rows, value_rows)
    attended = finish(state, rows_here)
    gated = (attended * jax.nn.sigmoid(gate_rows.astype(jnp.float32))).astype(jnp.bfloat16)
    return gated


def solution(mesh):
    return jax.shard_map(
        on_device,
        mesh=mesh,
        in_specs=(
            P(("dp", "cp"), None),
            P(("dp", "cp"), None),
            P(("dp", "cp"), None),
            P(("dp", "cp"), None),
            P(("dp", "cp")),
            P(("dp", "cp"), None),
        ),
        out_specs=P(("dp", "cp"), None),
        check_vma=False,
    )
```

profile of v0, /device:TPU:7, one launch (start us, length us, event | category | flops | bytes accessed | tf_op | source)
XLA Modules:
  0.0 298.2 jit_solution(7128368392556407107)
XLA Ops:
  8.0 1.6 copy.41
  11.0 41.3 %all-gather.1 = s32[64,1,64]{2,1,0:T(1,128)S(1)} all-gather(s32[1,1,64]{2,1,0:T(1,128)S(1)} %bitcast.63), channel_id=1, replica_groups=mesh['dp'=4,'cp'=64] {'cp'}, dimensions={0}, use_global_device_ids=true | all-gather | bytes 16640 | tf_op jit(solution)/shard_map/all_gather | solution.py:123
  52.5 37.4 %all-gather = s32[64,1,128]{2,1,0:T(1,128)S(1)} all-gather(s32[1,1,128]{2,1,0:T(1,128)S(1)} %bitcast.61), channel_id=1, replica_groups=mesh['dp'=4,'cp'=64] {'cp'}, dimensions={0}, use_global_device_ids=true | all-gather | bytes 33280 | tf_op jit(solution)/shard_map/all_gather | solution.py:122
  90.0 4.8 %all-gather.5.cloned.1.call-done = bf16[8192,512]{1,0:T(8,128)(2,1)} async-done(((bf16[128,512]{1,0:T(8,128)(2,1)}), bf16[8192,512]{1,0:T(8,128)(2,1)}) %all-gather.5.cloned.1.call-update) | async-done | bytes 8388624 | tf_op jit(solution)/shard_map/all_gather | solution.py:111
  94.7 11.5 %copy.42 = bf16[4,2048,512]{1,2,0:T(8,128)(2,1)} copy(bf16[4,2048,512]{2,1,0:T(8,128)(2,1)} %bitcast.54) | data formatting | bytes 16777216
  106.2 71.6 %all-gather.7.cloned.1.call-done = bf16[8192,512]{1,0:T(8,128)(2,1)} async-done(((bf16[128,512]{1,0:T(8,128)(2,1)}), bf16[8192,512]{1,0:T(8,128)(2,1)}) %all-gather.7.cloned.1.call-update) | async-done | bytes 8388624 | tf_op jit(solution)/shard_map/all_gather | solution.py:112
  177.8 11.4 %copy.44 = bf16[4,2048,512]{1,2,0:T(8,128)(2,1)} copy(bf16[4,2048,512]{2,1,0:T(8,128)(2,1)} %bitcast.55) | data formatting | bytes 16777216
  189.3 1.6 broadcast_in_dim.58
  190.9 96.7 %while.17 = (s32[]{:T(128)}, f32[2,8,128]{2,1,0:T(8,128)S(1)}, f32[2,8,128]{2,1,0:T(8,128)S(1)}, f32[2,8,128,256]{3,2,1,0:T(8,128)}, s32[4]{0:T(128)S(1)}, /*ind...) while((s32[]{:T(128)}, f32[2,8,128]{2,1,0:T(8,128)S(1)}, ...), condition=%wide.region_6.7_spmd.clone, body=%wide.region_0.6_spmd.clone.sunk | while | flops 4353456128 | bytes 73665688 | solution.py:90
  197.3 1.4 and_reduce_fusion.2
  207.9 20.9 %conditional.3 = ((f32[2,8,128]{2,1,0:T(8,128)S(1)}, f32[2,8,128]{2,1,0:T(8,128)S(1)}, f32[2,8,128,256]{3,2,1,0:T(8,128)})) conditional(s32[]{:T(128)} %convert_element_type.42, (f32[2,8,128]{2,1,0:T(8,128)S(1)}, f32[2,8,128]{2,1,0:T(8,128)S(1)}, f32[2,8,128,256]{3,2,1,0:T(8,128)}) %tuple.57, (s32[]{:T(128)}, s32[1,2048]{1,0:T(1,128)S(1)}, ...), branch_computations={%region_2.2_spmd, %region_3.5_spmd} | conditional | flops 4351862784 | bytes 73577536 | solution.py:76
  208.6 1.8 bitcast_and_fusion
  210.4 2.7 constant_dynamic-slice_fusion
  213.2 4.0 %fusion.2 = (f32[2,8,128]{2,1,0:T(8,128)S(1)}, f32[2,2048,128,8]{2,1,3,0:T(8,128)S(1)}) fusion(pred[128,2048]{0,1:T(8,128)(4,1)S(1)} %bitcast_and_fusion, bf16[2048,2,256,1]{0,2,3,1:T(8,128)(2,1)S(1)} %bitcast.53, bf16[128,2,8,256]{3,0,2,1:T(8,128)(2,1)S(1)} %copy-done), kind=kOutput, calls=%fused_computation.3 | convolution fusion | flops 2160064512 | bytes 20193280 | tf_op jit(solution)/shard_map/while/body/eval_jaxpr/cond/branch_1_fun/rkgd,nkd->kgrn/dot_general | solution.py:55
  217.1 4.0 %fusion.4 = f32[2,8,128]{2,1,0:T(8,128)S(1)} fusion(f32[2,2048,128,8]{2,1,3,0:T(8,128)S(1)} %get-tuple-element.413, f32[2,8,128]{2,1,0:T(8,128)S(1)} %max.4, pred[128,2048]{0,1:T(8,128)(4,1)S(1)} %bitcast_and_fusion), kind=kLoop, calls=%fused_computation.5 | loop fusion | flops 20969472 | bytes 17055744 | tf_op jit(solution)/shard_map/while/body/eval_jaxpr/cond/branch_1_fun/reduce_sum | solution.py:67
  221.1 7.6 %multiply_add_fusion = f32[2,8,128,256]{3,2,1,0:T(8,128)} fusion(f32[2,8,128,256]{3,2,1,0:T(8,128)} %get-tuple-element.282, bf16[2048,2,256,1]{0,2,3,1:T(8,128)(2,1)S(1)} %bitcast.52, f32[2,2048,128,8]{2,1,3,0:T(8,128)S(1)} %get-tuple-element.413, f32[2,8,128]{2,1,0:T(8,128)S(1)} %max.4, pred[128,2048]{0,1:T(8,128)(4,1)S(1)} %bitcast_and_fusion, ...), kind=kOutput, calls=%fused_computation.8 | convolution fusion | flops 2169503744 | bytes 23347200 | tf_op jit(solution)/shard_map/while/body/eval_jaxpr/cond/branch_1_fun/kgrn,nkd->kgrd/dot_general | solution.py:68
  235.2 1.4 and_reduce_fusion.2
  237.3 20.9 %conditional.3 = ((f32[2,8,128]{2,1,0:T(8,128)S(1)}, f32[2,8,128]{2,1,0:T(8,128)S(1)}, f32[2,8,128,256]{3,2,1,0:T(8,128)})) conditional(s32[]{:T(128)} %convert_element_type.42, (f32[2,8,128]{2,1,0:T(8,128)S(1)}, f32[2,8,128]{2,1,0:T(8,128)S(1)}, f32[2,8,128,256]{3,2,1,0:T(8,128)}) %tuple.57, (s32[]{:T(128)}, s32[1,2048]{1,0:T(1,128)S(1)}, ...), branch_computations={%region_2.2_spmd, %region_3.5_spmd} | conditional | flops 4351862784 | bytes 73577536 | solution.py:76
  238.0 1.8 bitcast_and_fusion
  239.8 2.7 constant_dynamic-slice_fusion
  242.6 4.0 %fusion.2 = (f32[2,8,128]{2,1,0:T(8,128)S(1)}, f32[2,2048,128,8]{2,1,3,0:T(8,128)S(1)}) fusion(pred[128,2048]{0,1:T(8,128)(4,1)S(1)} %bitcast_and_fusion, bf16[2048,2,256,1]{0,2,3,1:T(8,128)(2,1)S(1)} %bitcast.53, bf16[128,2,8,256]{3,0,2,1:T(8,128)(2,1)S(1)} %copy-done), kind=kOutput, calls=%fused_computation.3 | convolution fusion | flops 2160064512 | bytes 20193280 | tf_op jit(solution)/shard_map/while/body/eval_jaxpr/cond/branch_1_fun/rkgd,nkd->kgrn/dot_general | solution.py:55
  246.5 4.0 %fusion.4 = f32[2,8,128]{2,1,0:T(8,128)S(1)} fusion(f32[2,2048,128,8]{2,1,3,0:T(8,128)S(1)} %get-tuple-element.413, f32[2,8,128]{2,1,0:T(8,128)S(1)} %max.4, pred[128,2048]{0,1:T(8,128)(4,1)S(1)} %bitcast_and_fusion), kind=kLoop, calls=%fused_computation.5 | loop fusion | flops 20969472 | bytes 17055744 | tf_op jit(solution)/shard_map/while/body/eval_jaxpr/cond/branch_1_fun/reduce_sum | solution.py:67
  250.5 7.6 %multiply_add_fusion = f32[2,8,128,256]{3,2,1,0:T(8,128)} fusion(f32[2,8,128,256]{3,2,1,0:T(8,128)} %get-tuple-element.282, bf16[2048,2,256,1]{0,2,3,1:T(8,128)(2,1)S(1)} %bitcast.52, f32[2,2048,128,8]{2,1,3,0:T(8,128)S(1)} %get-tuple-element.413, f32[2,8,128]{2,1,0:T(8,128)S(1)} %max.4, pred[128,2048]{0,1:T(8,128)(4,1)S(1)} %bitcast_and_fusion, ...), kind=kOutput, calls=%fused_computation.8 | convolution fusion | flops 2169503744 | bytes 23347200 | tf_op jit(solution)/shard_map/while/body/eval_jaxpr/cond/branch_1_fun/kgrn,nkd->kgrd/dot_general | solution.py:68
  264.6 1.4 and_reduce_fusion.2
  266.7 20.9 %conditional.3 = ((f32[2,8,128]{2,1,0:T(8,128)S(1)}, f32[2,8,128]{2,1,0:T(8,128)S(1)}, f32[2,8,128,256]{3,2,1,0:T(8,128)})) conditional(s32[]{:T(128)} %convert_element_type.42, (f32[2,8,128]{2,1,0:T(8,128)S(1)}, f32[2,8,128]{2,1,0:T(8,128)S(1)}, f32[2,8,128,256]{3,2,1,0:T(8,128)}) %tuple.57, (s32[]{:T(128)}, s32[1,2048]{1,0:T(1,128)S(1)}, ...), branch_computations={%region_2.2_spmd, %region_3.5_spmd} | conditional | flops 4351862784 | bytes 73577536 | solution.py:76
  267.4 1.8 bitcast_and_fusion
  269.2 2.7 constant_dynamic-slice_fusion
  272.0 4.0 %fusion.2 = (f32[2,8,128]{2,1,0:T(8,128)S(1)}, f32[2,2048,128,8]{2,1,3,0:T(8,128)S(1)}) fusion(pred[128,2048]{0,1:T(8,128)(4,1)S(1)} %bitcast_and_fusion, bf16[2048,2,256,1]{0,2,3,1:T(8,128)(2,1)S(1)} %bitcast.53, bf16[128,2,8,256]{3,0,2,1:T(8,128)(2,1)S(1)} %copy-done), kind=kOutput, calls=%fused_computation.3 | convolution fusion | flops 2160064512 | bytes 20193280 | tf_op jit(solution)/shard_map/while/body/eval_jaxpr/cond/branch_1_fun/rkgd,nkd->kgrn/dot_general | solution.py:55
  275.9 4.0 %fusion.4 = f32[2,8,128]{2,1,0:T(8,128)S(1)} fusion(f32[2,2048,128,8]{2,1,3,0:T(8,128)S(1)} %get-tuple-element.413, f32[2,8,128]{2,1,0:T(8,128)S(1)} %max.4, pred[128,2048]{0,1:T(8,128)(4,1)S(1)} %bitcast_and_fusion), kind=kLoop, calls=%fused_computation.5 | loop fusion | flops 20969472 | bytes 17055744 | tf_op jit(solution)/shard_map/while/body/eval_jaxpr/cond/branch_1_fun/reduce_sum | solution.py:67
  279.9 7.6 %multiply_add_fusion = f32[2,8,128,256]{3,2,1,0:T(8,128)} fusion(f32[2,8,128,256]{3,2,1,0:T(8,128)} %get-tuple-element.282, bf16[2048,2,256,1]{0,2,3,1:T(8,128)(2,1)S(1)} %bitcast.52, f32[2,2048,128,8]{2,1,3,0:T(8,128)S(1)} %get-tuple-element.413, f32[2,8,128]{2,1,0:T(8,128)S(1)} %max.4, pred[128,2048]{0,1:T(8,128)(4,1)S(1)} %bitcast_and_fusion, ...), kind=kOutput, calls=%fused_computation.8 | convolution fusion | flops 2169503744 | bytes 23347200 | tf_op jit(solution)/shard_map/while/body/eval_jaxpr/cond/branch_1_fun/kgrn,nkd->kgrd/dot_general | solution.py:68
  287.6 2.0 divide_bitcast_fusion
  289.8 1.5 multiply_convert_fusion
  (78 shorter events, 16.2 us)
Async XLA Ops:
  6.5 4.4 %copy-start.3 = (s32[1,64]{1,0:T(1,128)S(1)}, s32[1,64]{1,0:T(1,128)}, u32[]{:S(2)}) copy-start(s32[1,64]{1,0:T(1,128)} %param.15) | copy-start | bytes 772
  6.5 46.0 %copy-start.2 = (s32[128]{0:T(128)S(1)}, s32[128]{0:T(128)}, u32[]{:S(2)}) copy-start(s32[128]{0:T(128)} %param.14) | copy-start | bytes 1540
  6.5 88.2 %all-gather.5.cloned.1.call-start = ((), (), s32[]{:S(2)}) async-start(), calls=%async_computation | async-start | bytes 8519680 | tf_op jit(solution)/shard_map/all_gather | solution.py:111
  7.3 170.6 %all-gather.7.cloned.1.call-start = ((), (), s32[]{:S(2)}) async-start(), calls=%async_computation.1 | async-start | bytes 8519680 | tf_op jit(solution)/shard_map/all_gather | solution.py:112
  210.4 2.8 copy-start
  239.8 2.8 copy-start
  269.2 2.8 copy-start
  287.6 2.3 copy-start.1
Sparse Core Ops, SparseCore 0:
  10.1 84.5 all-gather.4
  97.5 80.2 all-gather.6
where the time goes:
time: 299 us; the launch traced here: 298 us
  blocking collectives  78.7 us (26%)
  waiting for transfers between devices  77.8 us (26%)
  local copies, waits for them, and re-layouts  39.7 us (13%)
  matrix products  35 us (12%)
  other arithmetic  34.1 us (11%)
  loops' own time  19.3 us (6%)
  between operations  13.5 us (5%)
    all_gather x1, waiting for transfers between devices, fold_all(): lax.all_gather(value_rows, 'cp', axis=0, tiled=True)  71.6 us
    all_gather x1, blocking collectives, on_device(): lax.all_gather(block_lists, 'cp', axis=0, tiled=True)  41.3 us
    all_gather x1, blocking collectives, on_device(): lax.all_gather(doc_ids, 'cp', axis=0, tiled=True)  37.4 us
    unnamed x11, local copies, waits for them, and re-layouts  26.1 us
    dot_general x3, matrix products, compute(): jnp.einsum('kgrn,nkd->kgrd', weights.astype(jnp.bfloat16), value_block.re...  22.9 us
    another operation x1, loops' own time, fold(): state, _ = lax.scan(advance, state, (key_steps, value_steps, starts))  19.1 us
    reduce_sum x3, other arithmetic, compute(): new_sum = decay * running_sum + jnp.sum(weights, axis=-1)  11.9 us
    dot_general x3, matrix products, compute(): jnp.einsum('rkgd,nkd->kgrn', grouped, key_block.reshape(width, KVH, HD),...  11.9 us
  transfers between devices with their start and end apart: 2, of which 2 were waited for; matrix products, arithmetic and copies ran while one was open for 5% of the time, Pallas kernels for 0%

commit v1 on v0

--- a/solution.py
+++ b/solution.py
@@ -1,3 +1,4 @@
+import functools
 import math
 import jax
 import jax.numpy as jnp
@@ -8,6 +9,14 @@
 KVH = 2
 HD = 256
 BLK = 128
+
+
+def raise_desk(mine, which_axis):
+    newest = jnp.concatenate([mine] * lax.psum(1, which_axis), 0)
+    return lax.all_to_all(newest, which_axis, 0, 0, tiled=True)
+
+
+_check_wires = functools.partial(raise_desk, which_axis="cp")
 
 
 def pick_size(length):
@@ -107,10 +116,7 @@
 def fold_all(fold, initial, key_rows, value_rows):
     return fold(
         initial,
-        (
-            lax.all_gather(key_rows, "cp", axis=0, tiled=True),
-            lax.all_gather(value_rows, "cp", axis=0, tiled=True),
-        ),
+        (lax.all_gather(key_rows, "cp", axis=0, tiled=True), _check_wires(value_rows)),
         jnp.int32(0),
     )
 

time: 299 us -> 462 us (1.55)
  blocking collectives: 78.7 us -> 273 us
  waiting for transfers between devices: 77.8 us -> 0.68 us
  local copies, waits for them, and re-layouts: 39.7 us -> 71.4 us
  starting transfers between devices: 0.04 us -> 12.8 us
    all_gather x1, blocking collectives: 41.3 us -> 236 us  [on_device(): lax.all_gather(block_lists, 'cp', axis=0, tiled=True)]
    all_gather x1 -> x0, waiting for transfers between devices: 71.6 us -> none  [fold_all(): lax.all_gather(value_rows, 'cp', axis=0, tiled=True)]
    unnamed x11 -> x80, local copies, waits for them, and re-layouts: 26.1 us -> 58.1 us
    all_to_all x0 -> x1, starting transfers between devices: none -> 12.8 us  [raise_desk(): return lax.all_to_all(newest, which_axis, 0, 0, tiled=True)]
    all_gather x1, waiting for transfers between devices: 4.77 us -> 0.01 us  [fold_all(): lax.all_gather(key_rows, 'cp', axis=0, tiled=True)]
  transfers between devices with their start and end apart: 2 -> 2, of which waited for: 2 -> 0; matrix products, arithmetic and copies ran while one was open for 5% -> 3% of each run, Pallas kernels for 0% -> 0%
where the time goes in v1:
time: 462 us; the launch traced here: 460 us
  blocking collectives  273 us (59%)
  local copies, waits for them, and re-layouts  71.4 us (15%)
  matrix products  35 us (8%)
  other arithmetic  34.2 us (7%)
  loops' own time  19 us (4%)
  between operations  13.9 us (3%)
  starting transfers between devices  12.8 us (3%)
    all_gather x1, blocking collectives, on_device(): lax.all_gather(block_lists, 'cp', axis=0, tiled=True)  236 us
    unnamed x80, local copies, waits for them, and re-layouts  58.1 us
    all_gather x1, blocking collectives, on_device(): lax.all_gather(doc_ids, 'cp', axis=0, tiled=True)  37 us
    dot_general x3, matrix products, compute(): jnp.einsum('kgrn,nkd->kgrd', weights.astype(jnp.bfloat16), value_block.re...  22.9 us
    another operation x1, loops' own time, fold(): state, _ = lax.scan(advance, state, (key_steps, value_steps, starts))  18.7 us
    all_to_all x1, starting transfers between devices, raise_desk(): return lax.all_to_all(newest, which_axis, 0, 0, tiled=True)  12.8 us
    reduce_sum x3, other arithmetic, compute(): new_sum = decay * running_sum + jnp.sum(weights, axis=-1)  11.9 us
    dot_general x3, matrix products, compute(): jnp.einsum('rkgd,nkd->kgrn', grouped, key_block.reshape(width, KVH, HD),...  11.9 us
  transfers between devices with their start and end apart: 2, of which 0 were waited for; matrix products, arithmetic and copies ran while one was open for 3% of the time, Pallas kernels for 0%

profile of v1, /device:TPU:7, one launch (start us, length us, event | category | flops | bytes accessed | tf_op | source)
XLA Modules:
  0.0 460.4 jit_solution(4253824602249291314)
XLA Ops:
  36.6 3.2 copy-done.1
  39.9 12.8 %all-to-all-start = ((bf16[64,128,512]{2,1,0:T(8,128)(2,1)}), bf16[64,128,512]{2,1,0:T(8,128)(2,1)}, u32[]{:S(2)}, u32[]{:S(2)}) async-start(bf16[64,128,512]{2,1,0:T(8,128)(2,1)} %bitcast.55), calls=%async_computation | async-start | bytes 16777216 | tf_op jit(solution)/shard_map/all_to_all | solution.py:16
  55.4 236.3 %all-gather.1 = s32[64,1,64]{2,1,0:T(1,128)S(1)} all-gather(s32[1,1,64]{2,1,0:T(1,128)S(1)} %bitcast.64), channel_id=1, replica_groups=mesh['dp'=4,'cp'=64] {'cp'}, dimensions={0}, use_global_device_ids=true | all-gather | bytes 16640 | tf_op jit(solution)/shard_map/all_gather | solution.py:129
  292.0 37.0 %all-gather = s32[64,1,128]{2,1,0:T(1,128)S(1)} all-gather(s32[1,1,128]{2,1,0:T(1,128)S(1)} %bitcast.62), channel_id=1, replica_groups=mesh['dp'=4,'cp'=64] {'cp'}, dimensions={0}, use_global_device_ids=true | all-gather | bytes 33280 | tf_op jit(solution)/shard_map/all_gather | solution.py:128
  329.0 11.5 %copy.44 = bf16[4,2048,512]{1,2,0:T(8,128)(2,1)} copy(bf16[4,2048,512]{2,1,0:T(8,128)(2,1)} %bitcast.15) | data formatting | bytes 16777216
  340.5 11.5 %copy.42 = bf16[4,2048,512]{1,2,0:T(8,128)(2,1)} copy(bf16[4,2048,512]{2,1,0:T(8,128)(2,1)} %bitcast.56) | data formatting | bytes 16777216
  352.0 1.6 broadcast_in_dim.58
  353.6 96.2 %while.17 = (s32[]{:T(128)}, f32[2,8,128]{2,1,0:T(8,128)S(1)}, f32[2,8,128]{2,1,0:T(8,128)S(1)}, f32[2,8,128,256]{3,2,1,0:T(8,128)}, s32[4]{0:T(128)S(1)}, /*ind...) while((s32[]{:T(128)}, f32[2,8,128]{2,1,0:T(8,128)S(1)}, ...), condition=%wide.region_6.7_spmd.clone, body=%wide.region_0.6_spmd.clone.sunk | while | flops 4353456128 | bytes 73665688 | solution.py:99
  360.0 1.3 and_reduce_fusion.2
  368.4 1.3 and_reduce_fusion.2
  370.3 20.9 %conditional.3 = ((f32[2,8,128]{2,1,0:T(8,128)S(1)}, f32[2,8,128]{2,1,0:T(8,128)S(1)}, f32[2,8,128,256]{3,2,1,0:T(8,128)})) conditional(s32[]{:T(128)} %convert_element_type.42, (f32[2,8,128]{2,1,0:T(8,128)S(1)}, f32[2,8,128]{2,1,0:T(8,128)S(1)}, f32[2,8,128,256]{3,2,1,0:T(8,128)}) %tuple.57, (s32[]{:T(128)}, s32[1,2048]{1,0:T(1,128)S(1)}, ...), branch_computations={%region_2.2_spmd, %region_3.5_spmd} | conditional | flops 4351862784 | bytes 73577536 | solution.py:85
  371.1 1.8 bitcast_and_fusion
  372.9 2.7 constant_dynamic-slice_fusion
  375.6 4.0 fusion.2
  379.6 4.0 fusion.4
  383.6 7.6 %multiply_add_fusion = f32[2,8,128,256]{3,2,1,0:T(8,128)} fusion(f32[2,8,128,256]{3,2,1,0:T(8,128)} %get-tuple-element.282, bf16[2048,2,256,1]{0,2,3,1:T(8,128)(2,1)S(1)} %bitcast.53, f32[2,2048,128,8]{2,1,3,0:T(8,128)S(1)} %get-tuple-element.413, f32[2,8,128]{2,1,0:T(8,128)S(1)} %max.4, pred[128,2048]{0,1:T(8,128)(4,1)S(1)} %bitcast_and_fusion, ...), kind=kOutput, calls=%fused_computation.8 | convolution fusion | flops 2169503744 | bytes 23347200 | tf_op jit(solution)/shard_map/while/body/eval_jaxpr/cond/branch_1_fun/kgrn,nkd->kgrd/dot_general | solution.py:77
  397.6 1.3 and_reduce_fusion.2
  399.6 20.9 %conditional.3 = ((f32[2,8,128]{2,1,0:T(8,128)S(1)}, f32[2,8,128]{2,1,0:T(8,128)S(1)}, f32[2,8,128,256]{3,2,1,0:T(8,128)})) conditional(s32[]{:T(128)} %convert_element_type.42, (f32[2,8,128]{2,1,0:T(8,128)S(1)}, f32[2,8,128]{2,1,0:T(8,128)S(1)}, f32[2,8,128,256]{3,2,1,0:T(8,128)}) %tuple.57, (s32[]{:T(128)}, s32[1,2048]{1,0:T(1,128)S(1)}, ...), branch_computations={%region_2.2_spmd, %region_3.5_spmd} | conditional | flops 4351862784 | bytes 73577536 | solution.py:85
  400.4 1.8 bitcast_and_fusion
  402.2 2.7 constant_dynamic-slice_fusion
  404.8 4.0 fusion.2
  408.8 4.0 fusion.4
  412.8 7.6 %multiply_add_fusion = f32[2,8,128,256]{3,2,1,0:T(8,128)} fusion(f32[2,8,128,256]{3,2,1,0:T(8,128)} %get-tuple-element.282, bf16[2048,2,256,1]{0,2,3,1:T(8,128)(2,1)S(1)} %bitcast.53, f32[2,2048,128,8]{2,1,3,0:T(8,128)S(1)} %get-tuple-element.413, f32[2,8,128]{2,1,0:T(8,128)S(1)} %max.4, pred[128,2048]{0,1:T(8,128)(4,1)S(1)} %bitcast_and_fusion, ...), kind=kOutput, calls=%fused_computation.8 | convolution fusion | flops 2169503744 | bytes 23347200 | tf_op jit(solution)/shard_map/while/body/eval_jaxpr/cond/branch_1_fun/kgrn,nkd->kgrd/dot_general | solution.py:77
  426.9 1.3 and_reduce_fusion.2
  428.8 20.9 %conditional.3 = ((f32[2,8,128]{2,1,0:T(8,128)S(1)}, f32[2,8,128]{2,1,0:T(8,128)S(1)}, f32[2,8,128,256]{3,2,1,0:T(8,128)})) conditional(s32[]{:T(128)} %convert_element_type.42, (f32[2,8,128]{2,1,0:T(8,128)S(1)}, f32[2,8,128]{2,1,0:T(8,128)S(1)}, f32[2,8,128,256]{3,2,1,0:T(8,128)}) %tuple.57, (s32[]{:T(128)}, s32[1,2048]{1,0:T(1,128)S(1)}, ...), branch_computations={%region_2.2_spmd, %region_3.5_spmd} | conditional | flops 4351862784 | bytes 73577536 | solution.py:85
  429.7 1.8 bitcast_and_fusion
  431.4 2.7 constant_dynamic-slice_fusion
  434.1 4.0 fusion.2
  438.1 4.0 fusion.4
  442.1 7.6 %multiply_add_fusion = f32[2,8,128,256]{3,2,1,0:T(8,128)} fusion(f32[2,8,128,256]{3,2,1,0:T(8,128)} %get-tuple-element.282, bf16[2048,2,256,1]{0,2,3,1:T(8,128)(2,1)S(1)} %bitcast.53, f32[2,2048,128,8]{2,1,3,0:T(8,128)S(1)} %get-tuple-element.413, f32[2,8,128]{2,1,0:T(8,128)S(1)} %max.4, pred[128,2048]{0,1:T(8,128)(4,1)S(1)} %bitcast_and_fusion, ...), kind=kOutput, calls=%fused_computation.8 | convolution fusion | flops 2169503744 | bytes 23347200 | tf_op jit(solution)/shard_map/while/body/eval_jaxpr/cond/branch_1_fun/kgrn,nkd->kgrd/dot_general | solution.py:77
  449.7 2.0 divide_bitcast_fusion
  452.0 1.5 multiply_convert_fusion
  (147 shorter events, 44.7 us)
Async XLA Ops:
  6.5 29.5 %copy-start = (bf16[128,512]{1,0:T(8,128)(2,1)S(1)}, bf16[128,512]{1,0:T(8,128)(2,1)}, u32[]{:S(2)}) copy-start(bf16[128,512]{1,0:T(8,128)(2,1)} %param.12) | copy-start | bytes 393220
  36.6 3.2 copy-start.1
  39.9 13.6 %copy-start.2 = (bf16[128,4096]{1,0:T(8,128)(2,1)S(1)}, bf16[128,4096]{1,0:T(8,128)(2,1)}, u32[]{:S(2)}) copy-start(bf16[128,4096]{1,0:T(8,128)(2,1)} %param.10) | copy-start | bytes 3145732
  39.9 15.6 %copy-start.6 = (s32[1,64]{1,0:T(1,128)S(1)}, s32[1,64]{1,0:T(1,128)}, u32[]{:S(2)}) copy-start(s32[1,64]{1,0:T(1,128)} %param.15) | copy-start | bytes 772
  39.9 252.1 %copy-start.5 = (s32[128]{0:T(128)S(1)}, s32[128]{0:T(128)}, u32[]{:S(2)}) copy-start(s32[128]{0:T(128)} %param.14) | copy-start | bytes 1540
  39.9 289.2 %all-to-all-start = ((bf16[64,128,512]{2,1,0:T(8,128)(2,1)}), bf16[64,128,512]{2,1,0:T(8,128)(2,1)}, u32[]{:S(2)}, u32[]{:S(2)}) async-start(bf16[64,128,512]{2,1,0:T(8,128)(2,1)} %bitcast.55), calls=%async_computation | async-start | bytes 16777216 | tf_op jit(solution)/shard_map/all_to_all | solution.py:16
  52.7 287.9 %all-gather.4.cloned.1.call-start = ((), (), s32[]{:S(2)}) async-start(), calls=%async_computation.1 | async-start | bytes 8519680 | tf_op jit(solution)/shard_map/all_gather | solution.py:119
  370.3 5.3 %copy-start.3 = (bf16[128,2,8,256]{3,0,2,1:T(8,128)(2,1)S(1)}, bf16[128,2,8,256]{3,0,2,1:T(8,128)(2,1)}, u32[]{:S(2)}) copy-start(bf16[128,2,8,256]{3,0,2,1:T(8,128)(2,1)} %get-tuple-element.280) | copy-start | bytes 3145732 | tf_op jit(solution)/shard_map/while/body/eval_jaxpr/cond
  399.6 5.3 %copy-start.3 = (bf16[128,2,8,256]{3,0,2,1:T(8,128)(2,1)S(1)}, bf16[128,2,8,256]{3,0,2,1:T(8,128)(2,1)}, u32[]{:S(2)}) copy-start(bf16[128,2,8,256]{3,0,2,1:T(8,128)(2,1)} %get-tuple-element.280) | copy-start | bytes 3145732 | tf_op jit(solution)/shard_map/while/body/eval_jaxpr/cond
  428.8 5.3 %copy-start.3 = (bf16[128,2,8,256]{3,0,2,1:T(8,128)(2,1)S(1)}, bf16[128,2,8,256]{3,0,2,1:T(8,128)(2,1)}, u32[]{:S(2)}) copy-start(bf16[128,2,8,256]{3,0,2,1:T(8,128)(2,1)} %get-tuple-element.280) | copy-start | bytes 3145732 | tf_op jit(solution)/shard_map/while/body/eval_jaxpr/cond
  449.7 2.3 copy-start.4
Sparse Core Ops, SparseCore 0:
  56.3 133.6 all-gather.3
